TPU v7x, 32 devices: a whole 2x2x4 slice. The times are simulated.
32 devices in a mesh: users: 16 (over z, y, core), heads: 2 (over x).
Axes of the slice: x: 2, y: 2, z: 4, core: 2. Of those that a mesh axis runs over, the one named last changes fastest.
Arguments:
- sessions: bfloat16 [8192, 4096], P(('users', 'heads')), parts along dimension 0, may hold values from -16 to 16
- input_weight: bfloat16 [3, 4096, 2048], P(None, None, 'heads'), may hold values from -1 to 1
- output_weight: bfloat16 [2048, 4096], P('heads'), may hold values from -0.359375 to 0.359375
- session_counts: int32 [32], P('users'), parts along dimension 0, may hold values from 1 to 384, 512 in all
Outputs:
- attended: bfloat16 [8192, 4096], P(('users', 'heads')), parts along dimension 0
There are 16 independent parts, one for each index of `users`. A program takes and returns all parts, laid end to end along the dimension named above; an argument that names none is the same for every part. Nothing has to cross between parts.
Inputs may be any that keep to these rules, and one draw needn't show every extreme that they name: `session_counts`: the 2 counts sum to 512.
All inputs are finite; a program needn't handle non-finite values.
Results may differ from a plain program's by a relative error of at most 0.015.
Values may be sent and summed in bfloat16 or wider, within the bound.
No kernel may reach another device: no remote copies, remote signals or barrier semaphores. Data moves between devices by JAX's collectives and lax.ppermute only.
A program may use at most 128 MiB of HBM per device.

v0:
```python
import jax
import jax.numpy as jnp
from jax import lax
from jax.sharding import PartitionSpec as P

HD = 128


def permitted(total, counts):
    positions = jnp.arange(total, dtype=jnp.int32)
    ends = jnp.cumsum(counts)
    row_user = jnp.sum((positions[:, None] >= ends[None, :]).astype(jnp.int32), axis=1)
    same_user = row_user[:, None] == row_user[None, :]
    return jnp.logical_and(same_user, positions[:, None] >= positions[None, :])


def attend(packed, allowed):
    total = packed.shape[1]
    width = packed.shape[2]
    block = min(512, total)
    count = total // block
    queries = packed[0].reshape(count, block, width // HD, HD)
    key_rows = packed[1].reshape(total, width // HD, HD)
    values = packed[2].reshape(total, width // HD, HD)
    masks = allowed.reshape(count, block, total)

    def one_block(pair):
        query_block, mask_block = pair
        scores = jnp.einsum(
            "qhe,khe->hqk", query_block, key_rows, preferred_element_type=jnp.float32
        ) * HD ** (-0.5)
        scores = jnp.where(mask_block[None], scores, -1e30)
        highest = jnp.max(scores, axis=2, keepdims=True)
        raised = jnp.where(mask_block[None], jnp.exp(scores - highest), 0.0)
        attn_probs = (raised / jnp.sum(raised, axis=2, keepdims=True)).astype(jnp.bfloat16)
        mixed = jnp.einsum("hqk,khe->qhe", attn_probs, values, preferred_element_type=jnp.float32)
        return mixed.astype(jnp.bfloat16).reshape(block, width)

    blocks_out = lax.map(one_block, (queries, masks))
    return blocks_out.reshape(total, width)


def per_device(sessions, input_weight, output_weight, session_counts):
    packed = jnp.einsum(
        "nd,cde->cne",
        lax.all_gather(sessions, "heads", axis=0, tiled=True),
        input_weight,
        preferred_element_type=jnp.float32,
    ).astype(jnp.bfloat16)
    total = packed.shape[1]
    allowed = permitted(total, session_counts)
    mixed = attend(packed, allowed)
    return lax.psum_scatter(
        jnp.dot(mixed, output_weight, preferred_element_type=jnp.float32).astype(jnp.bfloat16),
        "heads",
        scatter_dimension=0,
        tiled=True,
    )


def solution(mesh):
    in_specs = (P(("users", "heads"), None), P(None, None, "heads"), P("heads", None), P("users"))
    out_specs = P(("users", "heads"), None)
    return jax.shard_map(
        per_device, mesh=mesh, in_specs=in_specs, out_specs=out_specs, check_vma=False
    )
```

profile of v0, /device:TPU:0, one launch (start us, length us, event | category | flops | bytes accessed | tf_op | source)
XLA Modules:
  0.0 167.7 jit_solution(7120729407783168606)
XLA Ops:
  6.5 0.0 all-gather.2.cloned.1.call-start
  6.5 0.7 all-gather.2.cloned.1.call-update
  7.3 0.0 reduce-scatter.2.cloned.1.call-start
  7.3 0.8 reduce-window.8
  8.1 0.1 fusion.14
  8.2 0.2 fusion.11
  8.4 59.9 %all-gather.2.cloned.1.call-done = bf16[512,4096]{1,0:T(8,128)(2,1)} async-done(((bf16[256,4096]{1,0:T(8,128)(2,1)}), bf16[512,4096]{1,0:T(8,128)(2,1)}) %all-gather.2.cloned.1.call-update) | async-done | bytes 4194320 | tf_op jit(solution)/shard_map/all_gather | solution.py:46
  68.4 18.2 %convert_bitcast_fusion = bf16[3,512,1024]{1,2,0:T(8,128)(2,1)S(1)} fusion(bf16[3,4096,1024]{2,1,0:T(8,128)(2,1)} %param.5, bf16[512,4096]{1,0:T(8,128)(2,1)} %all-gather.2.cloned.1.call-done), kind=kOutput, calls=%fused_computation.12 | convolution fusion | flops 12886474752 | bytes 32505856 | tf_op jit(solution)/shard_map/nd,cde->cne/dot_general | solution.py:44
  86.6 0.2 fusion.17
  86.8 5.9 %fusion.18 = (f32[8,512]{1,0:T(8,128)S(1)}, f32[8,512,512]{1,2,0:T(8,128)}) fusion(pred[512,512]{0,1:T(8,128)(4,1)S(1)} %fusion.11, bf16[512,8,128]{0,2,1:T(8,128)(2,1)S(1)} %bitcast.25, bf16[512,8,128]{0,2,1:T(8,128)(2,1)S(1)} %bitcast.24), kind=kOutput, calls=%fused_computation.22 | convolution fusion | flops 547357184 | bytes 10764288 | tf_op jit(solution)/shard_map/while/body/eval_jaxpr/sub | solution.py:34
  92.7 4.1 %fusion.10 = bf16[8,128,512]{2,1,0:T(8,128)(2,1)S(1)} fusion(bf16[512,8,128]{0,2,1:T(8,128)(2,1)S(1)} %bitcast.23, f32[8,512,512]{1,2,0:T(8,128)} %get-tuple-element.26, f32[8,512]{1,0:T(8,128)S(1)} %get-tuple-element.24), kind=kOutput, calls=%fused_computation.13 | convolution fusion | flops 541589504 | bytes 10502144 | tf_op jit(solution)/shard_map/while/body/eval_jaxpr/hqk,khe->qhe/dot_general | solution.py:36
  96.8 9.5 %convolution_convert_fusion = bf16[512,4096]{1,0:T(8,128)(2,1)} fusion(bf16[512,1024]{0,1:T(8,128)(2,1)S(1)} %bitcast.28, bf16[1024,4096]{1,0:T(8,128)(2,1)} %param.6), kind=kOutput, calls=%fused_computation.5 | convolution fusion | flops 4297064448 | bytes 13631488 | tf_op jit(solution)/shard_map/dot_general | solution.py:54
  106.3 0.0 reduce-scatter.2.cloned.1.call-update
  106.4 54.5 %reduce-scatter.2.cloned.1.call-done = bf16[256,4096]{1,0:T(8,128)(2,1)} async-done(((bf16[512,4096]{1,0:T(8,128)(2,1)}), bf16[256,4096]{1,0:T(8,128)(2,1)}) %reduce-scatter.2.cloned.1.call-update) | async-done | bytes 2097168 | tf_op jit(solution)/shard_map/reduce_scatter | solution.py:53
Async XLA Ops:
  6.5 61.8 %all-gather.2.cloned.1.call-start = ((), (), s32[]{:S(2)}) async-start(), calls=%async_computation.1 | async-start | bytes 6291456 | tf_op jit(solution)/shard_map/all_gather | solution.py:46
  7.3 153.6 %reduce-scatter.2.cloned.1.call-start = ((), (), s32[]{:S(2)}) async-start(), calls=%async_computation.2 | async-start | bytes 6291456 | tf_op jit(solution)/shard_map/reduce_scatter | solution.py:53
Sparse Core Ops, SparseCore 0:
  8.9 59.4 all-gather.1
  106.5 54.3 reduce-scatter.1
where the time goes:
time: 168 us
  waiting for transfers between devices  115 us (68%)
  matrix products  37.8 us (22%)
  between operations  13.4 us (8%)
    all_gather x1, waiting for transfers between devices, per_device(): lax.all_gather(sessions, 'heads', axis=0, tiled=True)  59.9 us
    reduce_scatter x1, waiting for transfers between devices, per_device(): lax.psum_scatter(jnp.dot(mixed, output_weight, preferred_element_type=jnp...  54.5 us
    dot_general x1, matrix products, per_device(): jnp.einsum('nd,cde->cne', lax.all_gather(sessions, 'heads', axis=0, tiled...  18.2 us
    dot_general x1, matrix products, per_device(): jnp.dot(mixed, output_weight, preferred_element_type=jnp.float32)  9.48 us
    sub x1, matrix products, one_block(): raised = jnp.where(mask_block[None], jnp.exp(scores - highest), 0.0)  5.92 us
    dot_general x1, matrix products, one_block(): jnp.einsum('hqk,khe->qhe', attn_probs, values, preferred_element_type=jnp...  4.11 us
  transfers between devices with their start and end apart: 2, of which 2 were waited for; matrix products, arithmetic and copies ran while one was open for 1% of the time, Pallas kernels for 0%

commit v1 on v0

--- a/solution.py
+++ b/solution.py
@@ -4,6 +4,24 @@
 from jax.sharding import PartitionSpec as P
 
 HD = 128
+
+
+def work_around(shard, axis, dim, apply, out_dim):
+    peers, mine, extent = (lax.axis_size(axis), lax.axis_index(axis), shard.shape[dim])
+    right = [(i, (i + 1) % peers) for i in range(peers)]
+    held, out = (shard, None)
+    for lap in range(peers):
+        source = (mine - lap) % peers
+        coming = lax.ppermute(held, axis, right) if lap < peers - 1 else None
+        made = apply(held, source * extent)
+        length = made.shape[out_dim]
+        if out is None:
+            out = jnp.zeros(
+                (*made.shape[:out_dim], peers * length, *made.shape[out_dim + 1 :]), made.dtype
+            )
+        out = lax.dynamic_update_slice_in_dim(out, made, source * length, axis=out_dim)
+        held = coming
+    return out
 
 
 def permitted(total, counts):
@@ -41,11 +59,14 @@
 
 
 def per_device(sessions, input_weight, output_weight, session_counts):
-    packed = jnp.einsum(
-        "nd,cde->cne",
-        lax.all_gather(sessions, "heads", axis=0, tiled=True),
-        input_weight,
-        preferred_element_type=jnp.float32,
+    packed = work_around(
+        sessions,
+        "heads",
+        0,
+        lambda shard, offset: jnp.einsum(
+            "nd,cde->cne", shard, input_weight, preferred_element_type=jnp.float32
+        ),
+        1,
     ).astype(jnp.bfloat16)
     total = packed.shape[1]
     allowed = permitted(total, session_counts)

time: 168 us -> 150 us (0.89)
  waiting for transfers between devices: 115 us -> 88.2 us
  matrix products: 37.8 us -> 44.1 us
  starting transfers between devices: 0.04 us -> 2.97 us
    all_gather x1 -> x0, waiting for transfers between devices: 59.9 us -> none  [per_device(): lax.all_gather(sessions, 'heads', axis=0, tiled=True)]
    ppermute x0 -> x1, waiting for transfers between devices: none -> 32.2 us  [work_around(): coming = lax.ppermute(held, axis, right) if lap < peers - 1 else None]
    dot_general x1 -> x2, matrix products: 18.2 us -> 24.5 us  [per_device(): jnp.einsum('nd,cde->cne', shard, input_weight, preferred_element_type=jnp...]
    ppermute x0 -> x1, starting transfers between devices: none -> 2.97 us  [work_around(): coming = lax.ppermute(held, axis, right) if lap < peers - 1 else None]
  transfers between devices with their start and end apart: 2 -> 2, of which waited for: 2 -> 2; matrix products, arithmetic and copies ran while one was open for 1% -> 9% of each run, Pallas kernels for 0% -> 0%
where the time goes in v1:
time: 150 us
  waiting for transfers between devices  88.2 us (59%)
  matrix products  44.1 us (29%)
  between operations  13.4 us (9%)
  starting transfers between devices  2.97 us (2%)
    reduce_scatter x1, waiting for transfers between devices, per_device(): lax.psum_scatter(jnp.dot(mixed, output_weight, preferred_element_type=jnp...  56 us
    ppermute x1, waiting for transfers between devices, work_around(): coming = lax.ppermute(held, axis, right) if lap < peers - 1 else None  32.2 us
    dot_general x2, matrix products, per_device(): jnp.einsum('nd,cde->cne', shard, input_weight, preferred_element_type=jnp...  24.5 us
    dot_general x1, matrix products, per_device(): jnp.dot(mixed, output_weight, preferred_element_type=jnp.float32)  9.48 us
    sub x1, matrix products, one_block(): raised = jnp.where(mask_block[None], jnp.exp(scores - highest), 0.0)  5.92 us
    dot_general x1, matrix products, one_block(): jnp.einsum('hqk,khe->qhe', attn_probs, values, preferred_element_type=jnp...  4.11 us
  transfers between devices with their start and end apart: 2, of which 2 were waited for; matrix products, arithmetic and copies ran while one was open for 9% of the time, Pallas kernels for 0%

profile of v1, /device:TPU:0, one launch (start us, length us, event | category | flops | bytes accessed | tf_op | source)
XLA Modules:
  0.0 150.3 jit_solution(16657075340059103853)
XLA Ops:
  6.5 0.0 reduce-scatter.2.cloned.1.call-start
  6.5 3.0 %collective-permute-start = (bf16[256,4096]{1,0:T(8,128)(2,1)}, bf16[256,4096]{1,0:T(8,128)(2,1)S(1)}, u32[]{:S(2)}, u32[]{:S(2)}) collective-permute-start(bf16[256,4096]{1,0:T(8,128)(2,1)} %param.4), channel_id=1, source_target_pairs={{0,1},{1,0},{2,3},{3,2},{4,5},{5,4},{6,7},{7,6},{8,9},{9,8},{10,11... | collective-permute-start | bytes 6291464 | tf_op jit(solution)/shard_map/ppermute | solution.py:15
  9.5 0.8 reduce-window.8
  10.3 0.1 fusion.18
  10.4 0.2 fusion.15
  10.6 0.2 broadcast_in_dim.42
  10.9 12.3 %bitcast_dynamic-update-slice_fusion.1 = bf16[3,512,1024]{1,2,0:T(8,128)(2,1)S(1)} fusion(bf16[3,512,1024]{1,2,0:T(8,128)(2,1)S(1)} %broadcast_in_dim.42, s32[]{:T(128)S(6)} %select_n.27, bf16[3,4096,1024]{2,1,0:T(8,128)(2,1)} %param.5, bf16[256,4096]{1,0:T(8,128)(2,1)} %param.4), kind=kOutput, calls=%fused_computation.11 | convolution fusion | flops 6442450944 | bytes 30408708 | tf_op jit(solution)/shard_map/nd,cde->cne/dot_general | solution.py:66
  23.2 32.2 %collective-permute-done = bf16[256,4096]{1,0:T(8,128)(2,1)S(1)} collective-permute-done((bf16[256,4096]{1,0:T(8,128)(2,1)}, bf16[256,4096]{1,0:T(8,128)(2,1)S(1)}, u32[]{:S(2)}, u32[]{:S(2)}) %collective-permute-start) | collective-permute-done | bytes 2097184 | tf_op jit(solution)/shard_map/ppermute | solution.py:15
  55.3 12.3 %bitcast_dynamic-update-slice_fusion = bf16[3,512,1024]{1,2,0:T(8,128)(2,1)S(1)} fusion(bf16[3,512,1024]{1,2,0:T(8,128)(2,1)S(1)} %bitcast_dynamic-update-slice_fusion.1, s32[]{:T(128)S(6)} %select_n.29, bf16[3,4096,1024]{2,1,0:T(8,128)(2,1)} %param.5, bf16[256,4096]{1,0:T(8,128)(2,1)S(1)} %collective-permute-done), kind=kOutput, calls=%fused_computation.10 | convolution fusion | flops 6442450944 | bytes 30408708 | tf_op jit(solution)/shard_map/nd,cde->cne/dot_general | solution.py:66
  67.6 0.3 fusion.21
  67.9 5.9 %fusion.22 = (f32[8,512]{1,0:T(8,128)S(1)}, f32[8,512,512]{1,2,0:T(8,128)}) fusion(pred[512,512]{0,1:T(8,128)(4,1)S(1)} %fusion.15, bf16[512,8,128]{0,2,1:T(8,128)(2,1)S(1)} %bitcast.33, bf16[512,8,128]{0,2,1:T(8,128)(2,1)S(1)} %bitcast.32), kind=kOutput, calls=%fused_computation.25 | convolution fusion | flops 547357184 | bytes 10764288 | tf_op jit(solution)/shard_map/while/body/eval_jaxpr/sub | solution.py:52
  73.8 4.1 %fusion.14 = bf16[8,128,512]{2,1,0:T(8,128)(2,1)S(1)} fusion(bf16[512,8,128]{0,2,1:T(8,128)(2,1)S(1)} %bitcast.31, f32[8,512,512]{1,2,0:T(8,128)} %get-tuple-element.26, f32[8,512]{1,0:T(8,128)S(1)} %get-tuple-element.24), kind=kOutput, calls=%fused_computation.16 | convolution fusion | flops 541589504 | bytes 10502144 | tf_op jit(solution)/shard_map/while/body/eval_jaxpr/hqk,khe->qhe/dot_general | solution.py:54
  77.9 9.5 %convolution_convert_fusion = bf16[512,4096]{1,0:T(8,128)(2,1)} fusion(bf16[512,1024]{0,1:T(8,128)(2,1)S(1)} %bitcast.36, bf16[1024,4096]{1,0:T(8,128)(2,1)} %param.6), kind=kOutput, calls=%fused_computation.5 | convolution fusion | flops 4297064448 | bytes 13631488 | tf_op jit(solution)/shard_map/dot_general | solution.py:75
  87.4 0.0 reduce-scatter.2.cloned.1.call-update
  87.4 56.0 %reduce-scatter.2.cloned.1.call-done = bf16[256,4096]{1,0:T(8,128)(2,1)} async-done(((bf16[512,4096]{1,0:T(8,128)(2,1)}), bf16[256,4096]{1,0:T(8,128)(2,1)}) %reduce-scatter.2.cloned.1.call-update) | async-done | bytes 2097168 | tf_op jit(solution)/shard_map/reduce_scatter | solution.py:74
Async XLA Ops:
  6.5 136.9 %reduce-scatter.2.cloned.1.call-start = ((), (), s32[]{:S(2)}) async-start(), calls=%async_computation.1 | async-start | bytes 6291456 | tf_op jit(solution)/shard_map/reduce_scatter | solution.py:74
  6.5 48.8 %collective-permute-start = (bf16[256,4096]{1,0:T(8,128)(2,1)}, bf16[256,4096]{1,0:T(8,128)(2,1)S(1)}, u32[]{:S(2)}, u32[]{:S(2)}) collective-permute-start(bf16[256,4096]{1,0:T(8,128)(2,1)} %param.4), channel_id=1, source_target_pairs={{0,1},{1,0},{2,3},{3,2},{4,5},{5,4},{6,7},{7,6},{8,9},{9,8},{10,11... | collective-permute-start | bytes 6291464 | tf_op jit(solution)/shard_map/ppermute | solution.py:15
Sparse Core Ops, SparseCore 0:
  87.6 55.8 reduce-scatter.1
